TPU v7x, 32 devices: a whole 2x2x4 slice. The times are simulated.
32 devices in a mesh: row: 8 (over y, x, core), col: 4 (over z).
Axes of the slice: x: 2, y: 2, z: 4, core: 2. Of those that a mesh axis runs over, the one named last changes fastest.
Arguments:
- features: bfloat16 [512, 128, 128], P('row', 'col'), may hold values from -6 to 6
- cotangent: bfloat16 [512, 128, 128], P('row', 'col'), may hold values from -6 to 6
- kernels: bfloat16 [2, 9, 128, 128], replicated, may hold values from -0.1875 to 0.1875
- momentum: float32 [2, 147456], replicated, may hold values from -6 to 6
- mlp_in_weight: float32 [32, 3], replicated, may hold values from -3.5 to 3.5
- mlp_in_bias: float32 [32], replicated, may hold values from -3 to 3
- mlp_out_weight: float32 [2, 32], replicated, may hold values from -1 to 1
- mlp_out_bias: float32 [2], replicated, may hold values from -3 to 3
Outputs:
- update: float32 [2, 147456], replicated
- momentum_out: float32 [2, 147456], replicated
All inputs are finite; a program needn't handle non-finite values.
Results may differ from a plain program's by a relative error of at most 0.0014.
Values may be sent and summed in bfloat16 or wider, within the bound.
A program may use at most 64 MiB of HBM per device.

v0:
```python
import math
import jax
import jax.numpy as jnp
from jax import lax
from jax.sharding import PartitionSpec as P


def padded_2(cells, sides, width):
    for axis, dim in sides:
        count = lax.axis_size(axis)
        head = lax.slice_in_dim(cells, 0, width, axis=dim)
        tail = lax.slice_in_dim(cells, cells.shape[dim] - width, cells.shape[dim], axis=dim)
        cells = jnp.concatenate(
            [
                lax.ppermute(tail, axis, [(i, (i + 1) % count) for i in range(count)]),
                cells,
                lax.ppermute(head, axis, [((i + 1) % count, i) for i in range(count)]),
            ],
            axis=dim,
        )
    return cells


def convolve(padded, kernel, tile_rows, tile_cols):
    channels = padded.shape[-1]
    summed = jnp.zeros((tile_rows * tile_cols, kernel.shape[-1]), jnp.float32)
    for tap_row in range(3):
        for tap_col in range(3):
            window = padded[tap_row : tap_row + tile_rows, tap_col : tap_col + tile_cols].reshape(
                tile_rows * tile_cols, channels
            )
            summed = summed + jnp.dot(
                window, kernel[3 * tap_row + tap_col], preferred_element_type=jnp.float32
            )
    return summed.reshape(tile_rows, tile_cols, -1)


def kernel_grad(padded, cotangent, tile_rows, tile_cols):
    channels = padded.shape[-1]
    flat_cot = cotangent.reshape(tile_rows * tile_cols, -1)
    taps = []
    for tap_row in range(3):
        for tap_col in range(3):
            window = padded[tap_row : tap_row + tile_rows, tap_col : tap_col + tile_cols].reshape(
                tile_rows * tile_cols, channels
            )
            taps.append(
                lax.dot_general(
                    window, flat_cot, (((0,), (0,)), ((), ())), preferred_element_type=jnp.float32
                )
            )
    return jnp.stack(taps)


def transpose_conv(cot_pad, kernel, tile_rows, tile_cols):
    channels = cot_pad.shape[-1]
    summed = jnp.zeros((tile_rows * tile_cols, kernel.shape[-2]), jnp.float32)
    for tap_row in range(3):
        for tap_col in range(3):
            window = cot_pad[
                2 - tap_row : 2 - tap_row + tile_rows, 2 - tap_col : 2 - tap_col + tile_cols
            ].reshape(tile_rows * tile_cols, channels)
            summed = summed + lax.dot_general(
                window,
                kernel[3 * tap_row + tap_col],
                (((1,), (1,)), ((), ())),
                preferred_element_type=jnp.float32,
            )
    return summed.reshape(tile_rows, tile_cols, -1)


def learned_step(grads, squares, momentum, weights, w_in, b_in, w_out, b_out, gain, count):
    norm_scale = 1.0 / jnp.sqrt(squares / count + 1e-06)
    g_hat = grads * norm_scale[:, None]
    momentum_new = 0.9 * momentum + 0.1 * g_hat
    scaled = weights.astype(jnp.float32) * gain
    pre_units = (
        w_in[:, 0][:, None, None] * g_hat[None] + w_in[:, 1][:, None, None] * momentum_new[None]
    )
    pre_units = pre_units + w_in[:, 2][:, None, None] * scaled[None] + b_in[:, None, None]
    units = jax.nn.silu(pre_units)
    mlp_result = (
        jnp.einsum("kh,hlp->klp", w_out, units, precision=lax.Precision.HIGHEST)
        + b_out[:, None, None]
    )
    update = mlp_result[0] * jnp.exp(jnp.tanh(mlp_result[1]))
    return (update, momentum_new)


def on_device(
    features, cotangent, kernels, momentum, mlp_in_weight, mlp_in_bias, mlp_out_weight, mlp_out_bias
):
    tile_rows, tile_cols, channels = features.shape
    param_count = 9 * channels * channels
    image_pad = padded_2(features, (("row", 0), ("col", 1)), 1)
    pre_act = convolve(image_pad, kernels[0], tile_rows, tile_cols)
    hidden = jax.nn.silu(pre_act).astype(jnp.bfloat16)
    hidden_pad = padded_2(hidden, (("row", 0), ("col", 1)), 1)
    cot_pad = padded_2(cotangent, (("row", 0), ("col", 1)), 1)
    grad_two = kernel_grad(hidden_pad, cotangent, tile_rows, tile_cols)
    back_grad = transpose_conv(cot_pad, kernels[1], tile_rows, tile_cols)
    sigma_val = jax.nn.sigmoid(pre_act)
    pre_grad = (back_grad * sigma_val * (1.0 + pre_act * (1.0 - sigma_val))).astype(jnp.bfloat16)
    grad_one = kernel_grad(image_pad, pre_grad, tile_rows, tile_cols)
    local_grads = jnp.stack([grad_one.reshape(-1), grad_two.reshape(-1)])
    weights = kernels.reshape(2, param_count)
    gain = math.sqrt(9.0 * channels)
    grads = lax.psum(local_grads, ("row", "col"))
    squares = jnp.sum(grads * grads, axis=1)
    update, momentum_out = learned_step(
        grads,
        squares,
        momentum,
        weights,
        mlp_in_weight,
        mlp_in_bias,
        mlp_out_weight,
        mlp_out_bias,
        gain,
        float(param_count),
    )
    return (update, momentum_out)


def solution(mesh):
    placed = (P("row", "col", None), P("row", "col", None), P(), P(), P(), P(), P(), P())
    return jax.shard_map(
        on_device, mesh=mesh, in_specs=placed, out_specs=(P(), P()), check_vma=False
    )
```

profile of v0, /device:TPU:0, one launch (start us, length us, event | category | flops | bytes accessed | tf_op | source)
XLA Modules:
  0.0 238.4 jit_solution(3576847353787842551)
XLA Ops:
  7.2 1.3 copy.30
  8.6 0.5 collective-permute-start
  9.1 2.9 %collective-permute-start.1 = (bf16[1,32,128]{2,0,1:T(2,128)(2,1)S(1)}, bf16[1,32,128]{2,0,1:T(2,128)(2,1)S(1)}, u32[]{:S(2)}, u32[]{:S(2)}) collective-permute-start(bf16[1,32,128]{2,0,1:T(2,128)(2,1)S(1)} %get-tuple-element.41), channel_id=1, source_target_pairs={{4,0},{8,4},{12,8},{16,12},{20,16},{24,20},{28,24},{0,28},{5,1},{9... | collective-permute-start | bytes 24584 | tf_op jit(solution)/shard_map/ppermute | solution.py:17
  12.1 0.7 fusion.119
  12.8 2.6 %collective-permute-start.4 = (bf16[1,32,128]{2,1,0:T(8,128)(2,1)S(1)}, bf16[1,32,128]{2,1,0:T(8,128)(2,1)S(1)}, u32[]{:S(2)}, u32[]{:S(2)}) collective-permute-start(bf16[1,32,128]{2,1,0:T(8,128)(2,1)S(1)} %get-tuple-element.34), channel_id=1, source_target_pairs={{4,0},{8,4},{12,8},{16,12},{20,16},{24,20},{28,24},{0,28},{5,1},{9... | collective-permute-start | bytes 24584 | tf_op jit(solution)/shard_map/ppermute | solution.py:17
  15.5 2.3 collective-permute-start.2
  17.8 2.1 collective-permute-start.7
  20.2 0.3 fusion.75
  20.5 0.3 fusion.68
  20.8 0.4 pad_maximum_fusion.7
  21.2 0.3 copy.35
  21.5 0.3 copy.41
  21.9 2.0 collective-permute-start.5
  23.9 0.5 collective-permute-start.6
  24.4 0.3 pad_maximum_fusion.1
  24.8 0.6 fusion.116
  25.4 0.3 copy.33
  26.0 0.3 copy.36
  26.4 0.3 copy.37
  26.7 0.3 copy.38
  27.1 0.3 copy.39
  27.4 0.3 copy.42
  27.8 2.3 collective-permute-done.6
  30.1 0.7 pad_maximum_fusion.11
  30.8 0.3 fusion.66
  32.0 0.7 copy-done.4
  34.2 0.3 convolution_add_fusion.14
  34.5 0.3 convolution_add_fusion.13
  34.8 0.3 convolution_add_fusion.12
  35.1 0.3 convolution_add_fusion.11
  35.4 0.3 convolution_add_fusion.10
  35.7 0.4 fusion.21
  36.0 1.4 fusion.43
  37.5 0.3 fusion.41
  37.8 0.3 fusion.40
  38.1 0.3 fusion.39
  38.5 0.3 fusion.38
  38.8 0.4 fusion.37
  39.2 0.3 fusion.36
  39.6 0.3 fusion.35
  40.1 2.6 %collective-permute-start.9 = (bf16[1,32,128]{2,0,1:T(2,128)(2,1)S(1)}, bf16[1,32,128]{2,0,1:T(2,128)(2,1)S(1)}, u32[]{:S(2)}, u32[]{:S(2)}) collective-permute-start(bf16[1,32,128]{2,0,1:T(2,128)(2,1)S(1)} %get-tuple-element.37), channel_id=1, source_target_pairs={{4,0},{8,4},{12,8},{16,12},{20,16},{24,20},{28,24},{0,28},{5,1},{9... | collective-permute-start | bytes 24584 | tf_op jit(solution)/shard_map/ppermute | solution.py:17
  42.7 0.3 fusion.34
  43.0 1.2 collective-permute-done.8
  44.3 4.0 %collective-permute-start.11 = (bf16[66,1,128]{2,0,1:T(8,128)(2,1)S(1)}, bf16[66,1,128]{2,0,1:T(8,128)(2,1)S(1)}, u32[]{:S(2)}, u32[]{:S(2)}) collective-permute-start(bf16[66,1,128]{2,0,1:T(8,128)(2,1)S(1)} %get-tuple-element.20), channel_id=1, source_target_pairs={{1,0},{2,1},{3,2},{0,3},{5,4},{6,5},{7,6},{4,7},{9,8},{10,9},{11,1... | collective-permute-start | bytes 50696 | tf_op jit(solution)/shard_map/ppermute | solution.py:17
  48.2 0.3 fusion.33
  48.6 1.2 collective-permute-done.10
  49.8 0.4 pad_maximum_fusion.2
  50.2 0.4 fusion.32
  50.6 0.5 fusion.31
  51.1 0.4 fusion.30
  51.4 0.4 fusion.29
  51.9 0.4 fusion.28
  52.3 0.4 fusion.27
  52.7 0.4 fusion.26
  53.2 0.5 fusion.25
  53.7 0.4 fusion.24
  54.1 1.9 pad_maximum_fusion
  56.2 4.3 %copy.91 = f32[1,2,1152,128]{3,1,2,0:T(2,128)S(1)} copy(f32[1,2,1152,128]{3,2,1,0:T(8,128)S(1)} %bitcast.218) | data formatting | bytes 2359296
  60.5 127.9 %all-reduce.2.cloned.1.call-done = f32[2,147456]{1,0:T(2,128)} async-done(((f32[2,147456]{1,0:T(2,128)}), f32[2,147456]{1,0:T(2,128)}) %all-reduce.2.cloned.1.call-update) | async-done | bytes 1179664 | tf_op jit(solution)/shard_map/psum | solution.py:108
  188.4 2.5 %multiply_reduce_fusion = f32[2]{0:T(128)S(1)} fusion(f32[2,147456]{1,0:T(2,128)} %all-reduce.2.cloned.1.call-done), kind=kLoop, calls=%fused_computation.45 | loop fusion | flops 589822 | bytes 1179656 | tf_op jit(solution)/shard_map/reduce_sum | solution.py:109
  191.0 1.3 multiply_add_fusion
  192.4 33.7 %fusion = f32[2,2,147456]{2,0,1:T(2,128)S(1)} fusion(f32[32]{0:T(128)S(1)} %copy-done.8, f32[2,147456]{1,0:T(2,128)S(1)} %bitcast.239, f32[32]{0:T(128)S(1)} %get-tuple-element.43, f32[2,147456]{1,0:T(2,128)S(1)} %get-tuple-element.2, f32[32]{0:T(128)S(1)} %get-tuple-element.44, f32[2,147456]{1,0:T(2,128)S(1)} %get-tuple-element.3, ...), kind=kOutput, calls=%fused_computation.1 | convolution fusion | flops 321454080 | bytes 5899016 | tf_op jit(solution)/shard_map/kh,hlp->klp/dot_general | solution.py:83
  226.1 2.5 %fusion.23 = f32[1,2,147456]{2,0,1:T(1,128)S(1)} fusion(f32[2,2,147456]{2,0,1:T(2,128)S(1)} %fusion), kind=kLoop, calls=%fused_computation.40 | loop fusion | flops 294912 | bytes 3538944 | tf_op jit(solution)/shard_map/mul | solution.py:86
  228.6 2.7 %copy.92 = f32[1,2,147456]{2,1,0:T(2,128)} copy(f32[1,2,147456]{2,0,1:T(1,128)S(1)} %fusion.23) | data formatting | bytes 2359296
  (53 shorter events, 3.3 us)
Async XLA Ops:
  7.2 185.2 %copy-start = (f32[2,32]{1,0:T(2,128)S(1)}, f32[2,32]{1,0:T(2,128)}, u32[]{:S(2)}) copy-start(f32[2,32]{1,0:T(2,128)} %param.14) | copy-start | bytes 772
  7.2 12.7 %copy-start.3 = (bf16[64,32,128]{2,1,0:T(8,128)(2,1)S(1)}, bf16[64,32,128]{2,1,0:T(8,128)(2,1)}, u32[]{:S(2)}) copy-start(bf16[64,32,128]{2,1,0:T(8,128)(2,1)} %param.9) | copy-start | bytes 1572868
  7.2 181.2 %all-reduce.2.cloned.1.call-start = ((), (), s32[]{:S(2)}) async-start(), calls=%async_computation | async-start | bytes 2359296 | tf_op jit(solution)/shard_map/psum | solution.py:108
  8.6 6.8 %collective-permute-start = (bf16[1,32,128]{2,0,1:T(2,128)(2,1)S(1)}, bf16[1,32,128]{2,0,1:T(2,128)(2,1)S(1)}, u32[]{:S(2)}, u32[]{:S(2)}) collective-permute-start(bf16[1,32,128]{2,0,1:T(2,128)(2,1)S(1)} %get-tuple-element.40), channel_id=1, source_target_pairs={{0,4},{4,8},{8,12},{12,16},{16,20},{20,24},{24,28},{28,0},{1,5},{5... | collective-permute-start | bytes 24584 | tf_op jit(solution)/shard_map/ppermute | solution.py:15
  9.1 6.3 %collective-permute-start.1 = (bf16[1,32,128]{2,0,1:T(2,128)(2,1)S(1)}, bf16[1,32,128]{2,0,1:T(2,128)(2,1)S(1)}, u32[]{:S(2)}, u32[]{:S(2)}) collective-permute-start(bf16[1,32,128]{2,0,1:T(2,128)(2,1)S(1)} %get-tuple-element.41), channel_id=1, source_target_pairs={{4,0},{8,4},{12,8},{16,12},{20,16},{24,20},{28,24},{0,28},{5,1},{9... | collective-permute-start | bytes 24584 | tf_op jit(solution)/shard_map/ppermute | solution.py:17
  12.8 7.1 %collective-permute-start.3 = (bf16[1,32,128]{2,1,0:T(8,128)(2,1)S(1)}, bf16[1,32,128]{2,1,0:T(8,128)(2,1)S(1)}, u32[]{:S(2)}, u32[]{:S(2)}) collective-permute-start(bf16[1,32,128]{2,1,0:T(8,128)(2,1)S(1)} %get-tuple-element.35), channel_id=1, source_target_pairs={{0,4},{4,8},{8,12},{12,16},{16,20},{20,24},{24,28},{28,0},{1,5},{5... | collective-permute-start | bytes 24584 | tf_op jit(solution)/shard_map/ppermute | solution.py:15
  12.8 7.1 %collective-permute-start.4 = (bf16[1,32,128]{2,1,0:T(8,128)(2,1)S(1)}, bf16[1,32,128]{2,1,0:T(8,128)(2,1)S(1)}, u32[]{:S(2)}, u32[]{:S(2)}) collective-permute-start(bf16[1,32,128]{2,1,0:T(8,128)(2,1)S(1)} %get-tuple-element.34), channel_id=1, source_target_pairs={{4,0},{8,4},{12,8},{16,12},{20,16},{24,20},{28,24},{0,28},{5,1},{9... | collective-permute-start | bytes 24584 | tf_op jit(solution)/shard_map/ppermute | solution.py:17
  15.4 4.8 %copy-start.2 = (bf16[2,9,128,128]{3,2,1,0:T(8,128)(2,1)S(1)}, bf16[2,9,128,128]{3,2,1,0:T(8,128)(2,1)}, u32[]{:S(2)}) copy-start(bf16[2,9,128,128]{3,2,1,0:T(8,128)(2,1)} %param.10) | copy-start | bytes 1769476
  15.5 9.0 %collective-permute-start.2 = (bf16[66,1,128]{2,0,1:T(8,128)(2,1)S(1)}, bf16[66,1,128]{2,0,1:T(8,128)(2,1)S(1)}, u32[]{:S(2)}, u32[]{:S(2)}) collective-permute-start(bf16[66,1,128]{2,0,1:T(8,128)(2,1)S(1)} %get-tuple-element.25), channel_id=1, source_target_pairs={{0,1},{1,2},{2,3},{3,0},{4,5},{5,6},{6,7},{7,4},{8,9},{9,10},{10,1... | collective-permute-start | bytes 50696 | tf_op jit(solution)/shard_map/ppermute | solution.py:15
  17.8 6.6 %collective-permute-start.7 = (bf16[66,1,128]{2,0,1:T(8,128)(2,1)S(1)}, bf16[66,1,128]{2,0,1:T(8,128)(2,1)S(1)}, u32[]{:S(2)}, u32[]{:S(2)}) collective-permute-start(bf16[66,1,128]{2,0,1:T(8,128)(2,1)S(1)} %get-tuple-element.24), channel_id=1, source_target_pairs={{1,0},{2,1},{3,2},{0,3},{5,4},{6,5},{7,6},{4,7},{9,8},{10,9},{11,1... | collective-permute-start | bytes 50696 | tf_op jit(solution)/shard_map/ppermute | solution.py:17
  21.9 5.9 %collective-permute-start.5 = (bf16[66,1,128]{2,1,0:T(2,128)(2,1)S(1)}, bf16[66,1,128]{2,1,0:T(2,128)(2,1)S(1)}, u32[]{:S(2)}, u32[]{:S(2)}) collective-permute-start(bf16[66,1,128]{2,1,0:T(2,128)(2,1)S(1)} %get-tuple-element.29), channel_id=1, source_target_pairs={{1,0},{2,1},{3,2},{0,3},{5,4},{6,5},{7,6},{4,7},{9,8},{10,9},{11,1... | collective-permute-start | bytes 50696 | tf_op jit(solution)/shard_map/ppermute | solution.py:17
  23.9 6.2 %collective-permute-start.6 = (bf16[66,1,128]{2,1,0:T(2,128)(2,1)S(1)}, bf16[66,1,128]{2,1,0:T(2,128)(2,1)S(1)}, u32[]{:S(2)}, u32[]{:S(2)}) collective-permute-start(bf16[66,1,128]{2,1,0:T(2,128)(2,1)S(1)} %get-tuple-element.30), channel_id=1, source_target_pairs={{0,1},{1,2},{2,3},{3,0},{4,5},{5,6},{6,7},{7,4},{8,9},{9,10},{10,1... | collective-permute-start | bytes 50696 | tf_op jit(solution)/shard_map/ppermute | solution.py:15
  31.7 1.0 copy-start.4
  40.0 4.2 %collective-permute-start.8 = (bf16[1,32,128]{2,0,1:T(2,128)(2,1)S(1)}, bf16[1,32,128]{2,0,1:T(2,128)(2,1)S(1)}, u32[]{:S(2)}, u32[]{:S(2)}) collective-permute-start(bf16[1,32,128]{2,0,1:T(2,128)(2,1)S(1)} %get-tuple-element.36), channel_id=1, source_target_pairs={{0,4},{4,8},{8,12},{12,16},{16,20},{20,24},{24,28},{28,0},{1,5},{5... | collective-permute-start | bytes 24584 | tf_op jit(solution)/shard_map/ppermute | solution.py:15
  40.1 4.1 %collective-permute-start.9 = (bf16[1,32,128]{2,0,1:T(2,128)(2,1)S(1)}, bf16[1,32,128]{2,0,1:T(2,128)(2,1)S(1)}, u32[]{:S(2)}, u32[]{:S(2)}) collective-permute-start(bf16[1,32,128]{2,0,1:T(2,128)(2,1)S(1)} %get-tuple-element.37), channel_id=1, source_target_pairs={{4,0},{8,4},{12,8},{16,12},{20,16},{24,20},{28,24},{0,28},{5,1},{9... | collective-permute-start | bytes 24584 | tf_op jit(solution)/shard_map/ppermute | solution.py:17
  44.2 5.6 %collective-permute-start.10 = (bf16[66,1,128]{2,0,1:T(8,128)(2,1)S(1)}, bf16[66,1,128]{2,0,1:T(8,128)(2,1)S(1)}, u32[]{:S(2)}, u32[]{:S(2)}) collective-permute-start(bf16[66,1,128]{2,0,1:T(8,128)(2,1)S(1)} %get-tuple-element.21), channel_id=1, source_target_pairs={{0,1},{1,2},{2,3},{3,0},{4,5},{5,6},{6,7},{7,4},{8,9},{9,10},{10,1... | collective-permute-start | bytes 50696 | tf_op jit(solution)/shard_map/ppermute | solution.py:15
  44.3 5.5 %collective-permute-start.11 = (bf16[66,1,128]{2,0,1:T(8,128)(2,1)S(1)}, bf16[66,1,128]{2,0,1:T(8,128)(2,1)S(1)}, u32[]{:S(2)}, u32[]{:S(2)}) collective-permute-start(bf16[66,1,128]{2,0,1:T(8,128)(2,1)S(1)} %get-tuple-element.20), channel_id=1, source_target_pairs={{1,0},{2,1},{3,2},{0,3},{5,4},{6,5},{7,6},{4,7},{9,8},{10,9},{11,1... | collective-permute-start | bytes 50696 | tf_op jit(solution)/shard_map/ppermute | solution.py:17
  56.2 4.3 %copy-start.7 = (f32[32,3]{0,1:T(4,128)S(1)}, f32[32,3]{0,1:T(4,128)}, u32[]{:S(2)}) copy-start(f32[32,3]{0,1:T(4,128)} %param.12) | copy-start | bytes 1156
  56.2 134.7 %copy-start.5 = (f32[2,147456]{1,0:T(2,128)S(1)}, f32[2,147456]{1,0:T(2,128)}, u32[]{:S(2)}) copy-start(f32[2,147456]{1,0:T(2,128)} %param.11) | copy-start | bytes 3538948
  188.4 2.5 %copy-start.1 = (f32[2,147456]{1,0:T(2,128)S(1)}, f32[2,147456]{1,0:T(2,128)}, u32[]{:S(2)}) copy-start(f32[2,147456]{1,0:T(2,128)} %all-reduce.2.cloned.1.call-done) | copy-start | bytes 3538948
  190.9 1.4 copy-start.8
  191.0 1.4 copy-start.9
  192.3 33.8 %copy-start.6 = (f32[2,147456]{1,0:T(2,128)}, f32[2,147456]{1,0:T(2,128)S(1)}, u32[]{:S(2)}) copy-start(f32[2,147456]{1,0:T(2,128)S(1)} %get-tuple-element.2) | copy-start | bytes 3538948
Sparse Core Ops, SparseCore 0:
  56.2 132.2 all-reduce.1
where the time goes:
time: 241 us; the launch traced here: 238 us
  waiting for transfers between devices  133 us (55%)
  matrix products  46 us (19%)
  starting transfers between devices  19.8 us (8%)
  between operations  14.8 us (6%)
  local copies, waits for them, and re-layouts  13.3 us (6%)
  other arithmetic  11.9 us (5%)
    psum x1, waiting for transfers between devices, on_device(): grads = lax.psum(local_grads, ('row', 'col'))  128 us
    dot_general x1, matrix products, learned_step(): jnp.einsum('kh,hlp->klp', w_out, units, precision=lax.Precision.HIGHEST)  33.7 us
    ppermute x6, starting transfers between devices, padded_2(): lax.ppermute(head, axis, [((i + 1) % count, i) for i in range(count)])  16.3 us
    unnamed x24, local copies, waits for them, and re-layouts  9.07 us
    dot_general x18, matrix products, kernel_grad(): lax.dot_general(window, flat_cot, (((0,), (0,)), ((), ())), preferred_ele...  7.03 us
  transfers between devices with their start and end apart: 13, of which 4 were waited for; matrix products, arithmetic and copies ran while one was open for 5% of the time, Pallas kernels for 0%

commit v1 on v0

--- a/solution.py
+++ b/solution.py
@@ -105,7 +105,9 @@
     local_grads = jnp.stack([grad_one.reshape(-1), grad_two.reshape(-1)])
     weights = kernels.reshape(2, param_count)
     gain = math.sqrt(9.0 * channels)
-    grads = lax.psum(local_grads, ("row", "col"))
+    grads = local_grads
+    for name in ("row", "col"):
+        grads = lax.psum(grads, name)
     squares = jnp.sum(grads * grads, axis=1)
     update, momentum_out = learned_step(
         grads,

time: 241 us -> 225 us (0.934)
  waiting for transfers between devices: 133 us -> 115 us
    psum x1 -> x2, waiting for transfers between devices: 128 us -> 110 us  [on_device(): grads = lax.psum(grads, name)]
    unnamed x24 -> x26, local copies, waits for them, and re-layouts: 9.07 us -> 9.88 us
  transfers between devices with their start and end apart: 13 -> 14, of which waited for: 4 -> 5; matrix products, arithmetic and copies ran while one was open for 5% -> 5% of each run, Pallas kernels for 0% -> 0%
where the time goes in v1:
time: 225 us; the launch traced here: 222 us
  waiting for transfers between devices  115 us (51%)
  matrix products  46 us (20%)
  starting transfers between devices  19.8 us (9%)
  between operations  14.8 us (7%)
  local copies, waits for them, and re-layouts  14.2 us (6%)
  other arithmetic  11.9 us (5%)
    psum x2, waiting for transfers between devices, on_device(): grads = lax.psum(grads, name)  110 us
    dot_general x1, matrix products, learned_step(): jnp.einsum('kh,hlp->klp', w_out, units, precision=lax.Precision.HIGHEST)  33.7 us
    ppermute x6, starting transfers between devices, padded_2(): lax.ppermute(head, axis, [((i + 1) % count, i) for i in range(count)])  16.3 us
    unnamed x26, local copies, waits for them, and re-layouts  9.88 us
    dot_general x18, matrix products, kernel_grad(): lax.dot_general(window, flat_cot, (((0,), (0,)), ((), ())), preferred_ele...  7.02 us
    ppermute x6, waiting for transfers between devices, padded_2(): lax.ppermute(tail, axis, [(i, (i + 1) % count) for i in range(count)])  4.59 us
  transfers between devices with their start and end apart: 14, of which 5 were waited for; matrix products, arithmetic and copies ran while one was open for 5% of the time, Pallas kernels for 0%

profile of v1, /device:TPU:0, one launch (start us, length us, event | category | flops | bytes accessed | tf_op | source)
XLA Modules:
  0.0 221.7 jit_solution(6491871045853965267)
XLA Ops:
  7.2 1.3 copy.30
  8.6 0.5 collective-permute-start
  9.1 2.9 %collective-permute-start.1 = (bf16[1,32,128]{2,0,1:T(2,128)(2,1)S(1)}, bf16[1,32,128]{2,0,1:T(2,128)(2,1)S(1)}, u32[]{:S(2)}, u32[]{:S(2)}) collective-permute-start(bf16[1,32,128]{2,0,1:T(2,128)(2,1)S(1)} %get-tuple-element.41), channel_id=1, source_target_pairs={{4,0},{8,4},{12,8},{16,12},{20,16},{24,20},{28,24},{0,28},{5,1},{9... | collective-permute-start | bytes 24584 | tf_op jit(solution)/shard_map/ppermute | solution.py:17
  12.1 0.7 fusion.119
  12.8 2.6 %collective-permute-start.4 = (bf16[1,32,128]{2,1,0:T(8,128)(2,1)S(1)}, bf16[1,32,128]{2,1,0:T(8,128)(2,1)S(1)}, u32[]{:S(2)}, u32[]{:S(2)}) collective-permute-start(bf16[1,32,128]{2,1,0:T(8,128)(2,1)S(1)} %get-tuple-element.34), channel_id=1, source_target_pairs={{4,0},{8,4},{12,8},{16,12},{20,16},{24,20},{28,24},{0,28},{5,1},{9... | collective-permute-start | bytes 24584 | tf_op jit(solution)/shard_map/ppermute | solution.py:17
  15.5 2.3 %collective-permute-start.2 = (bf16[66,1,128]{2,0,1:T(8,128)(2,1)S(1)}, bf16[66,1,128]{2,0,1:T(8,128)(2,1)S(1)}, u32[]{:S(2)}, u32[]{:S(2)}) collective-permute-start(bf16[66,1,128]{2,0,1:T(8,128)(2,1)S(1)} %get-tuple-element.25), channel_id=1, source_target_pairs={{0,1},{1,2},{2,3},{3,0},{4,5},{5,6},{6,7},{7,4},{8,9},{9,10},{10,1... | collective-permute-start | bytes 50696 | tf_op jit(solution)/shard_map/ppermute | solution.py:15
  17.8 2.1 collective-permute-start.7
  20.3 0.3 fusion.75
  20.6 0.3 fusion.68
  20.9 0.4 pad_maximum_fusion.7
  21.3 0.3 copy.35
  21.6 0.3 copy.41
  22.0 2.0 collective-permute-start.5
  23.9 0.5 collective-permute-start.6
  24.5 0.4 pad_maximum_fusion.1
  24.8 0.7 fusion.116
  25.6 0.3 copy.33
  26.2 0.3 copy.36
  26.5 0.3 copy.37
  26.9 0.3 copy.38
  27.2 0.3 copy.39
  27.6 0.3 copy.42
  27.9 2.2 collective-permute-done.6
  30.1 0.7 pad_maximum_fusion.11
  30.9 0.3 fusion.66
  32.0 0.7 copy-done.4
  34.2 0.3 convolution_add_fusion.14
  34.5 0.3 convolution_add_fusion.13
  34.8 0.3 convolution_add_fusion.12
  35.1 0.3 convolution_add_fusion.11
  35.7 0.4 fusion.21
  36.1 1.4 fusion.43
  37.5 0.3 fusion.41
  37.9 0.4 fusion.40
  38.2 0.3 fusion.39
  38.6 0.3 fusion.38
  38.9 0.4 fusion.37
  39.3 0.3 fusion.36
  39.7 0.3 fusion.35
  40.1 2.6 %collective-permute-start.9 = (bf16[1,32,128]{2,0,1:T(2,128)(2,1)S(1)}, bf16[1,32,128]{2,0,1:T(2,128)(2,1)S(1)}, u32[]{:S(2)}, u32[]{:S(2)}) collective-permute-start(bf16[1,32,128]{2,0,1:T(2,128)(2,1)S(1)} %get-tuple-element.37), channel_id=1, source_target_pairs={{4,0},{8,4},{12,8},{16,12},{20,16},{24,20},{28,24},{0,28},{5,1},{9... | collective-permute-start | bytes 24584 | tf_op jit(solution)/shard_map/ppermute | solution.py:17
  42.7 0.3 fusion.34
  43.1 1.2 collective-permute-done.8
  44.4 4.0 %collective-permute-start.11 = (bf16[66,1,128]{2,0,1:T(8,128)(2,1)S(1)}, bf16[66,1,128]{2,0,1:T(8,128)(2,1)S(1)}, u32[]{:S(2)}, u32[]{:S(2)}) collective-permute-start(bf16[66,1,128]{2,0,1:T(8,128)(2,1)S(1)} %get-tuple-element.20), channel_id=1, source_target_pairs={{1,0},{2,1},{3,2},{0,3},{5,4},{6,5},{7,6},{4,7},{9,8},{10,9},{11,1... | collective-permute-start | bytes 50696 | tf_op jit(solution)/shard_map/ppermute | solution.py:17
  48.3 0.3 fusion.33
  48.7 1.2 collective-permute-done.10
  49.9 0.4 pad_maximum_fusion.2
  50.3 0.4 fusion.32
  50.7 0.5 fusion.31
  51.1 0.4 fusion.30
  51.5 0.5 fusion.29
  52.0 0.4 fusion.28
  52.4 0.4 fusion.27
  52.8 0.4 fusion.26
  53.3 0.5 fusion.25
  53.7 0.4 fusion.24
  54.2 1.9 pad_maximum_fusion
  56.2 57.9 %all-reduce.3.cloned.1.call-done = f32[2,147456]{1,0:T(2,128)} async-done(((f32[2,147456]{1,0:T(2,128)}), f32[2,147456]{1,0:T(2,128)}) %all-reduce.3.cloned.1.call-update) | async-done | bytes 1179664 | tf_op jit(solution)/shard_map/psum | solution.py:110
  114.3 5.1 %copy.91 = f32[1,2,1152,128]{3,1,2,0:T(2,128)} copy(f32[1,2,1152,128]{3,2,1,0:T(8,128)S(1)} %bitcast.218) | data formatting | bytes 2359296
  119.4 52.3 %all-reduce.5.cloned.1.call-done = f32[2,147456]{1,0:T(2,128)} async-done(((f32[2,147456]{1,0:T(2,128)}), f32[2,147456]{1,0:T(2,128)}) %all-reduce.5.cloned.1.call-update) | async-done | bytes 1179664 | tf_op jit(solution)/shard_map/psum | solution.py:110
  171.7 2.5 %multiply_reduce_fusion = f32[2]{0:T(128)S(1)} fusion(f32[2,147456]{1,0:T(2,128)} %all-reduce.5.cloned.1.call-done), kind=kLoop, calls=%fused_computation.45 | loop fusion | flops 589822 | bytes 1179656 | tf_op jit(solution)/shard_map/reduce_sum | solution.py:111
  174.3 1.4 multiply_add_fusion
  175.7 33.7 %fusion = f32[2,2,147456]{2,0,1:T(2,128)S(1)} fusion(f32[32]{0:T(128)S(1)} %copy-done.9, f32[2,147456]{1,0:T(2,128)S(1)} %bitcast.239, f32[32]{0:T(128)S(1)} %get-tuple-element.43, f32[2,147456]{1,0:T(2,128)S(1)} %get-tuple-element.2, f32[32]{0:T(128)S(1)} %get-tuple-element.44, f32[2,147456]{1,0:T(2,128)S(1)} %get-tuple-element.3, ...), kind=kOutput, calls=%fused_computation.1 | convolution fusion | flops 321454080 | bytes 5899016 | tf_op jit(solution)/shard_map/kh,hlp->klp/dot_general | solution.py:83
  209.4 2.5 %fusion.23 = f32[1,2,147456]{2,0,1:T(1,128)S(1)} fusion(f32[2,2,147456]{2,0,1:T(2,128)S(1)} %fusion), kind=kLoop, calls=%fused_computation.40 | loop fusion | flops 294912 | bytes 3538944 | tf_op jit(solution)/shard_map/mul | solution.py:86
  212.0 2.7 %copy.92 = f32[1,2,147456]{2,1,0:T(2,128)} copy(f32[1,2,147456]{2,0,1:T(1,128)S(1)} %fusion.23) | data formatting | bytes 2359296
  (58 shorter events, 3.7 us)
Async XLA Ops:
  7.2 168.5 %copy-start = (f32[2,32]{1,0:T(2,128)S(1)}, f32[2,32]{1,0:T(2,128)}, u32[]{:S(2)}) copy-start(f32[2,32]{1,0:T(2,128)} %param.14) | copy-start | bytes 772
  7.2 12.7 %copy-start.3 = (bf16[64,32,128]{2,1,0:T(8,128)(2,1)S(1)}, bf16[64,32,128]{2,1,0:T(8,128)(2,1)}, u32[]{:S(2)}) copy-start(bf16[64,32,128]{2,1,0:T(8,128)(2,1)} %param.9) | copy-start | bytes 1572868
  7.2 106.9 %all-reduce.3.cloned.1.call-start = ((), (), s32[]{:S(2)}) async-start(), calls=%async_computation | async-start | bytes 2359296 | tf_op jit(solution)/shard_map/psum | solution.py:110
  8.6 6.8 %collective-permute-start = (bf16[1,32,128]{2,0,1:T(2,128)(2,1)S(1)}, bf16[1,32,128]{2,0,1:T(2,128)(2,1)S(1)}, u32[]{:S(2)}, u32[]{:S(2)}) collective-permute-start(bf16[1,32,128]{2,0,1:T(2,128)(2,1)S(1)} %get-tuple-element.40), channel_id=1, source_target_pairs={{0,4},{4,8},{8,12},{12,16},{16,20},{20,24},{24,28},{28,0},{1,5},{5... | collective-permute-start | bytes 24584 | tf_op jit(solution)/shard_map/ppermute | solution.py:15
  9.1 6.3 %collective-permute-start.1 = (bf16[1,32,128]{2,0,1:T(2,128)(2,1)S(1)}, bf16[1,32,128]{2,0,1:T(2,128)(2,1)S(1)}, u32[]{:S(2)}, u32[]{:S(2)}) collective-permute-start(bf16[1,32,128]{2,0,1:T(2,128)(2,1)S(1)} %get-tuple-element.41), channel_id=1, source_target_pairs={{4,0},{8,4},{12,8},{16,12},{20,16},{24,20},{28,24},{0,28},{5,1},{9... | collective-permute-start | bytes 24584 | tf_op jit(solution)/shard_map/ppermute | solution.py:17
  12.8 7.1 %collective-permute-start.3 = (bf16[1,32,128]{2,1,0:T(8,128)(2,1)S(1)}, bf16[1,32,128]{2,1,0:T(8,128)(2,1)S(1)}, u32[]{:S(2)}, u32[]{:S(2)}) collective-permute-start(bf16[1,32,128]{2,1,0:T(8,128)(2,1)S(1)} %get-tuple-element.35), channel_id=1, source_target_pairs={{0,4},{4,8},{8,12},{12,16},{16,20},{20,24},{24,28},{28,0},{1,5},{5... | collective-permute-start | bytes 24584 | tf_op jit(solution)/shard_map/ppermute | solution.py:15
  12.8 7.1 %collective-permute-start.4 = (bf16[1,32,128]{2,1,0:T(8,128)(2,1)S(1)}, bf16[1,32,128]{2,1,0:T(8,128)(2,1)S(1)}, u32[]{:S(2)}, u32[]{:S(2)}) collective-permute-start(bf16[1,32,128]{2,1,0:T(8,128)(2,1)S(1)} %get-tuple-element.34), channel_id=1, source_target_pairs={{4,0},{8,4},{12,8},{16,12},{20,16},{24,20},{28,24},{0,28},{5,1},{9... | collective-permute-start | bytes 24584 | tf_op jit(solution)/shard_map/ppermute | solution.py:17
  15.4 4.8 %copy-start.2 = (bf16[2,9,128,128]{3,2,1,0:T(8,128)(2,1)S(1)}, bf16[2,9,128,128]{3,2,1,0:T(8,128)(2,1)}, u32[]{:S(2)}) copy-start(bf16[2,9,128,128]{3,2,1,0:T(8,128)(2,1)} %param.10) | copy-start | bytes 1769476
  15.5 9.0 %collective-permute-start.2 = (bf16[66,1,128]{2,0,1:T(8,128)(2,1)S(1)}, bf16[66,1,128]{2,0,1:T(8,128)(2,1)S(1)}, u32[]{:S(2)}, u32[]{:S(2)}) collective-permute-start(bf16[66,1,128]{2,0,1:T(8,128)(2,1)S(1)} %get-tuple-element.25), channel_id=1, source_target_pairs={{0,1},{1,2},{2,3},{3,0},{4,5},{5,6},{6,7},{7,4},{8,9},{9,10},{10,1... | collective-permute-start | bytes 50696 | tf_op jit(solution)/shard_map/ppermute | solution.py:15
  17.8 6.7 %collective-permute-start.7 = (bf16[66,1,128]{2,0,1:T(8,128)(2,1)S(1)}, bf16[66,1,128]{2,0,1:T(8,128)(2,1)S(1)}, u32[]{:S(2)}, u32[]{:S(2)}) collective-permute-start(bf16[66,1,128]{2,0,1:T(8,128)(2,1)S(1)} %get-tuple-element.24), channel_id=1, source_target_pairs={{1,0},{2,1},{3,2},{0,3},{5,4},{6,5},{7,6},{4,7},{9,8},{10,9},{11,1... | collective-permute-start | bytes 50696 | tf_op jit(solution)/shard_map/ppermute | solution.py:17
  22.0 6.0 %collective-permute-start.5 = (bf16[66,1,128]{2,1,0:T(2,128)(2,1)S(1)}, bf16[66,1,128]{2,1,0:T(2,128)(2,1)S(1)}, u32[]{:S(2)}, u32[]{:S(2)}) collective-permute-start(bf16[66,1,128]{2,1,0:T(2,128)(2,1)S(1)} %get-tuple-element.29), channel_id=1, source_target_pairs={{1,0},{2,1},{3,2},{0,3},{5,4},{6,5},{7,6},{4,7},{9,8},{10,9},{11,1... | collective-permute-start | bytes 50696 | tf_op jit(solution)/shard_map/ppermute | solution.py:17
  23.9 6.2 %collective-permute-start.6 = (bf16[66,1,128]{2,1,0:T(2,128)(2,1)S(1)}, bf16[66,1,128]{2,1,0:T(2,128)(2,1)S(1)}, u32[]{:S(2)}, u32[]{:S(2)}) collective-permute-start(bf16[66,1,128]{2,1,0:T(2,128)(2,1)S(1)} %get-tuple-element.30), channel_id=1, source_target_pairs={{0,1},{1,2},{2,3},{3,0},{4,5},{5,6},{6,7},{7,4},{8,9},{9,10},{10,1... | collective-permute-start | bytes 50696 | tf_op jit(solution)/shard_map/ppermute | solution.py:15
  31.7 1.0 copy-start.4
  40.0 4.2 %collective-permute-start.8 = (bf16[1,32,128]{2,0,1:T(2,128)(2,1)S(1)}, bf16[1,32,128]{2,0,1:T(2,128)(2,1)S(1)}, u32[]{:S(2)}, u32[]{:S(2)}) collective-permute-start(bf16[1,32,128]{2,0,1:T(2,128)(2,1)S(1)} %get-tuple-element.36), channel_id=1, source_target_pairs={{0,4},{4,8},{8,12},{12,16},{16,20},{20,24},{24,28},{28,0},{1,5},{5... | collective-permute-start | bytes 24584 | tf_op jit(solution)/shard_map/ppermute | solution.py:15
  40.1 4.2 %collective-permute-start.9 = (bf16[1,32,128]{2,0,1:T(2,128)(2,1)S(1)}, bf16[1,32,128]{2,0,1:T(2,128)(2,1)S(1)}, u32[]{:S(2)}, u32[]{:S(2)}) collective-permute-start(bf16[1,32,128]{2,0,1:T(2,128)(2,1)S(1)} %get-tuple-element.37), channel_id=1, source_target_pairs={{4,0},{8,4},{12,8},{16,12},{20,16},{24,20},{28,24},{0,28},{5,1},{9... | collective-permute-start | bytes 24584 | tf_op jit(solution)/shard_map/ppermute | solution.py:17
  44.3 5.6 %collective-permute-start.10 = (bf16[66,1,128]{2,0,1:T(8,128)(2,1)S(1)}, bf16[66,1,128]{2,0,1:T(8,128)(2,1)S(1)}, u32[]{:S(2)}, u32[]{:S(2)}) collective-permute-start(bf16[66,1,128]{2,0,1:T(8,128)(2,1)S(1)} %get-tuple-element.21), channel_id=1, source_target_pairs={{0,1},{1,2},{2,3},{3,0},{4,5},{5,6},{6,7},{7,4},{8,9},{9,10},{10,1... | collective-permute-start | bytes 50696 | tf_op jit(solution)/shard_map/ppermute | solution.py:15
  44.4 5.5 %collective-permute-start.11 = (bf16[66,1,128]{2,0,1:T(8,128)(2,1)S(1)}, bf16[66,1,128]{2,0,1:T(8,128)(2,1)S(1)}, u32[]{:S(2)}, u32[]{:S(2)}) collective-permute-start(bf16[66,1,128]{2,0,1:T(8,128)(2,1)S(1)} %get-tuple-element.20), channel_id=1, source_target_pairs={{1,0},{2,1},{3,2},{0,3},{5,4},{6,5},{7,6},{4,7},{9,8},{10,9},{11,1... | collective-permute-start | bytes 50696 | tf_op jit(solution)/shard_map/ppermute | solution.py:17
  56.1 115.6 %all-reduce.5.cloned.1.call-start = ((), (), s32[]{:S(2)}) async-start(), calls=%async_computation.1 | async-start | bytes 2359296 | tf_op jit(solution)/shard_map/psum | solution.py:110
  114.3 5.1 %copy-start.8 = (f32[32,3]{0,1:T(4,128)S(1)}, f32[32,3]{0,1:T(4,128)}, u32[]{:S(2)}) copy-start(f32[32,3]{0,1:T(4,128)} %param.12) | copy-start | bytes 1156
  114.3 60.0 %copy-start.5 = (f32[2,147456]{1,0:T(2,128)S(1)}, f32[2,147456]{1,0:T(2,128)}, u32[]{:S(2)}) copy-start(f32[2,147456]{1,0:T(2,128)} %param.11) | copy-start | bytes 3538948
  171.7 2.5 %copy-start.1 = (f32[2,147456]{1,0:T(2,128)S(1)}, f32[2,147456]{1,0:T(2,128)}, u32[]{:S(2)}) copy-start(f32[2,147456]{1,0:T(2,128)} %all-reduce.5.cloned.1.call-done) | copy-start | bytes 3538948
  174.3 1.4 copy-start.7
  174.3 1.4 copy-start.9
  174.3 1.4 copy-start.10
  175.7 33.8 %copy-start.6 = (f32[2,147456]{1,0:T(2,128)}, f32[2,147456]{1,0:T(2,128)S(1)}, u32[]{:S(2)}) copy-start(f32[2,147456]{1,0:T(2,128)S(1)} %get-tuple-element.2) | copy-start | bytes 3538948
Sparse Core Ops, SparseCore 0:
  56.2 57.8 all-reduce.2
  116.5 55.2 all-reduce.4
